TPU v7x, 32 devices: a whole 2x2x4 slice. The times are simulated.
32 devices in a mesh: pop: 8 (over z, x), mp: 4 (over y, core).
Axes of the slice: x: 2, y: 2, z: 4, core: 2. Of those that a mesh axis runs over, the one named last changes fastest.
Arguments:
- context: bfloat16 [3072, 5120], P('pop', 'mp'), may hold values from -9 to 9
- out_weight: bfloat16 [5120, 5120], P('mp'), may hold values from -0.078125 to 0.078125
- residual: bfloat16 [3072, 5120], P('pop', 'mp'), may hold values from -6 to 6
- target: bfloat16 [3072, 5120], P('pop', 'mp'), may hold values from -9 to 9
- norm_gain: float32 [5120], replicated, may hold values from 0.5 to 1.5
- left_factors: bfloat16 [128, 5120], P('pop'), may hold values from -6 to 6
- right_factors: bfloat16 [128, 5120], P('pop'), may hold values from -8 to 8
- member_ranks: int32 [128], P('pop'), may hold values from 0 to 127, each once
Outputs:
- update: float32 [5120, 5120], P('pop', 'mp')
- fitness: float32 [128], P('pop')
- base: float32 [3072, 5120], P('pop', 'mp')
Inputs may be any that keep to these rules, and one draw needn't show every extreme that they name: `member_ranks`: each number from 0 to 127 appears exactly once.
All inputs are finite; a program needn't handle non-finite values.
Results may differ from a plain program's by a relative error of at most 0.0095.
Values may be sent and summed in bfloat16 or wider, within the bound.
A program may use at most 64 MiB of HBM per device.

v0:
```python
import math

import jax
import jax.numpy as jnp
from jax import lax
from jax.sharding import PartitionSpec as P

SIGMA = 1.0
EPSILON = 1e-06


def error_sums(stream, lifted, right_rows, gain_part, target_rows, inverse):
    hidden = stream[:, None, :] + lifted[:, :, None] * right_rows[None, :, :]
    differ = gain_part * hidden * inverse[:, :, None] - target_rows[:, None, :]
    return jnp.sum(differ * differ, axis=(0, 2))


def utility(member_ranks, count_all):
    levels = jnp.arange(count_all).astype(jnp.float32)
    ceiling = math.log(count_all / 2 + 1)
    baseline = jnp.maximum(0.0, ceiling - jnp.log(levels + 1.0))
    shaped = jnp.maximum(0.0, ceiling - jnp.log(member_ranks.astype(jnp.float32) + 1.0))
    return shaped / jnp.sum(baseline) - 1.0 / count_all


def shards(
    context, out_weight, residual, target, norm_gain, left_factors, right_factors, member_ranks
):
    tok_count = context.shape[0]
    shard_width = context.shape[1]
    full_width = out_weight.shape[1]
    factor = SIGMA / math.sqrt(full_width)
    offset = lax.axis_index("mp") * shard_width
    left_cols = lax.dynamic_slice_in_dim(left_factors, offset, shard_width, 1)
    right_cols = lax.dynamic_slice_in_dim(right_factors, offset, shard_width, 1)
    partial_value = jnp.dot(context, out_weight, preferred_element_type=jnp.float32)
    projected = lax.dot_general(
        context, left_cols, (((1,), (1,)), ((), ())), preferred_element_type=jnp.float32
    )
    summed = lax.psum_scatter(
        partial_value.astype(jnp.bfloat16), "mp", scatter_dimension=1, tiled=True
    ).astype(jnp.float32)
    stream = residual.astype(jnp.float32) + summed
    gain_part = lax.dynamic_slice_in_dim(norm_gain, offset, shard_width, 0)
    factor_f = right_cols.astype(jnp.float32)
    crossed = jnp.dot(stream, factor_f.T, precision=lax.Precision.HIGHEST)
    per_token = jnp.sum(stream * stream, axis=1)
    per_member = jnp.sum(factor_f * factor_f, axis=1)
    projected, crossed, per_token, per_member = lax.psum(
        (projected, crossed, per_token, per_member), "mp"
    )
    lifted = factor * projected
    meansq = (
        per_token[:, None] + 2.0 * lifted * crossed + lifted * lifted * per_member[None, :]
    ) / full_width
    inverse = lax.rsqrt(meansq + EPSILON)
    local_error = error_sums(
        stream, lifted, factor_f, gain_part, target.astype(jnp.float32), inverse
    )
    member_total = lax.psum(local_error, "mp")
    fitness = -member_total / (tok_count * full_width)
    everyone = lax.all_gather(fitness, "pop", axis=0, tiled=True)
    count_all = everyone.shape[0]
    average = jnp.mean(everyone)
    centre = everyone - average
    spread = jnp.sqrt(jnp.mean(centre * centre) + 1e-05)
    weight = utility(member_ranks, count_all) + (fitness - average) / spread / count_all
    weighted = (weight[:, None] * left_factors.astype(jnp.float32)).astype(jnp.bfloat16)
    weighted_rows = lax.all_to_all(weighted, "pop", split_axis=1, concat_axis=0, tiled=True)
    right_all = lax.all_gather(right_cols, "pop", axis=0, tiled=True)
    update = lax.dot_general(
        weighted_rows, right_all, (((0,), (0,)), ((), ())), preferred_element_type=jnp.float32
    ) * (math.sqrt(count_all) / SIGMA)
    return (update, fitness, stream)


def solution(mesh):
    in_specs = (
        P("pop", "mp"),
        P("mp", None),
        P("pop", "mp"),
        P("pop", "mp"),
        P(),
        P("pop", None),
        P("pop", None),
        P("pop"),
    )
    out_specs = (P("pop", "mp"), P("pop"), P("pop", "mp"))
    return jax.shard_map(shards, mesh=mesh, in_specs=in_specs, out_specs=out_specs, check_vma=False)
```

profile of v0, /device:TPU:0, one launch (start us, length us, event | category | flops | bytes accessed | tf_op | source)
XLA Modules:
  0.0 169.2 jit_solution(15076576406600554811)
XLA Ops:
  7.2 0.0 copy-start
  7.2 0.0 copy-start.5
  7.2 0.0 copy-start.2
  7.2 0.0 reduce-scatter.2.cloned.1.call-start
  7.2 1.4 copy-done
  8.7 11.4 %convolution_convert_fusion = bf16[384,5120]{1,0:T(8,128)(2,1)} fusion(bf16[384,1280]{1,0:T(8,128)(2,1)S(1)} %copy-done, bf16[1280,5120]{1,0:T(8,128)(2,1)} %param.9), kind=kOutput, calls=%fused_computation.1 | convolution fusion | flops 5035130880 | bytes 18022400 | tf_op jit(solution)/shard_map/dot_general | solution.py:36
  20.1 0.0 reduce-scatter.2.cloned.1.call-update
  20.1 0.0 copy-start.4
  20.2 0.0 copy-done.2
  20.2 1.4 convert_element_type.33
  21.6 0.8 dynamic_slice.9
  22.4 0.0 copy-done.5
  22.4 0.6 dynamic-slice
  23.6 0.6 maximum_reduce_fusion
  24.2 0.8 fusion.3
  25.0 0.1 multiply_reduce_fusion.2
  25.1 1.1 convolution_bitcast_fusion
  26.2 39.6 %reduce-scatter.2.cloned.1.call-done = bf16[384,1280]{1,0:T(8,128)(2,1)} async-done(((bf16[384,5120]{1,0:T(8,128)(2,1)}), bf16[384,1280]{1,0:T(8,128)(2,1)}) %reduce-scatter.2.cloned.1.call-update) | async-done | bytes 983056 | tf_op jit(solution)/shard_map/reduce_scatter | solution.py:40
  65.8 1.9 %multiply_reduce_fusion.1 = (f32[384]{0:T(512)S(1)}, f32[384,1280]{1,0:T(8,128)S(1)}) fusion(bf16[384,1280]{1,0:T(8,128)(2,1)} %reduce-scatter.2.cloned.1.call-done, bf16[384,1280]{1,0:T(8,128)(2,1)} %param.10), kind=kLoop, calls=%fused_computation.3 | loop fusion | flops 2457216 | bytes 3933696 | tf_op jit(solution)/shard_map/reduce_sum | solution.py:47
  67.7 0.0 copy-start.1
  67.7 1.0 fusion.4
  68.7 10.7 %all-reduce.1 = (f32[384,16]{0,1:T(8,128)S(1)}, f32[384,16]{0,1:T(8,128)S(1)}, f32[16]{0:T(128)S(1)}, f32[384]{0:T(512)S(1)}) all-reduce(f32[384,16]{0,1:T(8,128)S(1)} %fusion.4, f32[384,16]{0,1:T(8,128)S(1)} %convolution_bitcast_fusion, f32[16]{0:T(128)S(1)} %multiply_reduce_fusion.2, ...), channel_id=1, replica_groups=mesh['pop'=8,'mp'=4] {'mp'}, use_global_device_ids=true, to_apply=%region_5.0 | all-reduce | flops 12688 | bytes 101504 | tf_op jit(solution)/shard_map/psum | solution.py:49
  79.4 0.1 broadcast_multiply_fusion
  79.5 0.1 copy.21
  79.6 0.1 copy.22
  79.8 12.8 %multiply_reduce_fusion = f32[16]{0:T(128)S(1)} fusion(f32[384,1280]{1,0:T(8,128)} %convert_element_type.33, f32[384,16]{1,0:T(8,128)S(1)} %copy.22, f32[16,1280]{1,0:T(8,128)S(1)} %get-tuple-element.9, f32[384,16]{1,0:T(8,128)S(1)} %copy.21, f32[384,1280]{1,0:T(8,128)S(1)} %get-tuple-element.12, f32[1280]{0:T(1024)S(1)} %dynamic_slice.9), kind=kLoop, calls=%fused_computation | loop fusion | flops 55050224 | bytes 4068416 | tf_op jit(solution)/shard_map/reduce_sum | solution.py:15
  92.5 5.8 %psum.39 = f32[16]{0:T(128)S(1)} all-reduce(f32[16]{0:T(128)S(1)} %multiply_reduce_fusion), channel_id=1, replica_groups=mesh['pop'=8,'mp'=4] {'mp'}, use_global_device_ids=true, to_apply=%region_9.0 | all-reduce | flops 16 | bytes 128 | tf_op jit(solution)/shard_map/psum | solution.py:60
  98.3 0.1 fusion.2
  98.4 0.0 copy-start.3
  98.4 21.5 %all-reduce = f32[128]{0:T(128)S(1)} all-reduce(f32[128]{0:T(128)S(1)} %get-tuple-element.7), channel_id=1, replica_groups=mesh['pop'=8,'mp'=4] {'pop'}, use_global_device_ids=true, to_apply=%add | all-reduce | flops 128 | bytes 1024
  119.9 0.6 reduce_sum.58
  121.1 0.6 multiply_reduce_fusion.3
  122.4 0.0 copy-done.4
  122.4 0.6 multiply_add_fusion
  123.0 1.0 multiply_convert_fusion
  124.0 0.7 copy.26
  124.7 3.4 %all-to-all-start = ((bf16[16,8,640]{2,0,1:T(8,128)(2,1)}), bf16[16,8,640]{2,0,1:T(8,128)(2,1)S(1)}, u32[]{:S(2)}, u32[]{:S(2)}) async-start(bf16[16,8,640]{2,0,1:T(8,128)(2,1)} %bitcast.16), calls=%async_computation.1 | async-start | bytes 327680 | tf_op jit(solution)/shard_map/all_to_all | solution.py:69
  128.1 31.9 %all_gather.7 = bf16[128,1280]{1,0:T(8,128)(2,1)S(1)} all-gather(bf16[16,1280]{1,0:T(8,128)(2,1)S(1)} %get-tuple-element.10), channel_id=1, replica_groups=mesh['pop'=8,'mp'=4] {'pop'}, dimensions={0}, use_global_device_ids=true | all-gather | bytes 368640 | tf_op jit(solution)/shard_map/all_gather | solution.py:70
  160.0 0.0 all-to-all-done
  160.0 2.3 %convolution_multiply_fusion = f32[640,1280]{1,0:T(8,128)} fusion(bf16[128,640]{1,0:T(8,128)(2,1)S(1)} %bitcast.17, bf16[128,1280]{1,0:T(8,128)(2,1)S(1)} %all_gather.7), kind=kOutput, calls=%fused_computation.2 | convolution fusion | flops 210534400 | bytes 3768320 | tf_op jit(solution)/shard_map/dot_general | solution.py:71
  162.4 0.0 copy-done.1
  162.4 0.0 copy-done.3
  (1 shorter events, 0.0 us)
Async XLA Ops:
  7.2 1.5 copy-start
  7.2 15.2 %copy-start.5 = (u32[32]{0:T(128)S(1)}, u32[32]{0:T(128)}, u32[]{:S(2)}) copy-start(u32[32]{0:T(128)} %constant.48) | copy-start | bytes 388
  7.2 13.0 %copy-start.2 = (bf16[384,1280]{1,0:T(8,128)(2,1)S(1)}, bf16[384,1280]{1,0:T(8,128)(2,1)}, u32[]{:S(2)}) copy-start(bf16[384,1280]{1,0:T(8,128)(2,1)} %param.11) | copy-start | bytes 2949124
  7.2 58.6 %reduce-scatter.2.cloned.1.call-start = ((), (), s32[]{:S(2)}) async-start(), calls=%async_computation.2 | async-start | bytes 4915200 | tf_op jit(solution)/shard_map/reduce_scatter | solution.py:40
  20.1 102.3 %copy-start.4 = (s32[16]{0:T(128)S(1)}, s32[16]{0:T(128)}, u32[]{:S(2)}) copy-start(s32[16]{0:T(128)} %param.15) | copy-start | bytes 196
  67.7 94.7 %copy-start.1 = (f32[384,1280]{1,0:T(8,128)}, f32[384,1280]{1,0:T(8,128)S(1)}, u32[]{:S(2)}) copy-start(f32[384,1280]{1,0:T(8,128)S(1)} %get-tuple-element.12) | copy-start | bytes 5898244
  98.4 64.0 %copy-start.3 = (f32[16]{0:T(128)}, f32[16]{0:T(128)S(1)}, u32[]{:S(2)}) copy-start(f32[16]{0:T(128)S(1)} %get-tuple-element.8) | copy-start | bytes 196
  124.7 35.3 %all-to-all-start = ((bf16[16,8,640]{2,0,1:T(8,128)(2,1)}), bf16[16,8,640]{2,0,1:T(8,128)(2,1)S(1)}, u32[]{:S(2)}, u32[]{:S(2)}) async-start(bf16[16,8,640]{2,0,1:T(8,128)(2,1)} %bitcast.16), calls=%async_computation.1 | async-start | bytes 327680 | tf_op jit(solution)/shard_map/all_to_all | solution.py:69
Sparse Core Ops, SparseCore 0:
  20.3 45.4 reduce-scatter.1
where the time goes:
time: 170 us; the launch traced here: 169 us
  blocking collectives  69.9 us (41%)
  waiting for transfers between devices  39.6 us (23%)
  other arithmetic  20.5 us (12%)
  between operations  16.1 us (9%)
  matrix products  15.9 us (9%)
  local copies, waits for them, and re-layouts  3.75 us (2%)
  starting transfers between devices  3.42 us (2%)
    reduce_scatter x1, waiting for transfers between devices, shards(): lax.psum_scatter(partial_value.astype(jnp.bfloat16), 'mp', scatter_dimens...  39.6 us
    all_gather x1, blocking collectives, shards(): right_all = lax.all_gather(right_cols, 'pop', axis=0, tiled=True)  31.9 us
    unnamed x1, blocking collectives  21.5 us
    reduce_sum x1, other arithmetic, error_sums(): return jnp.sum(differ * differ, axis=(0, 2))  12.8 us
    dot_general x1, matrix products, shards(): jnp.dot(context, out_weight, preferred_element_type=jnp.float32)  11.4 us
    psum x1, blocking collectives, shards(): lax.psum((projected, crossed, per_token, per_member), 'mp')  10.7 us
    psum x1, blocking collectives, shards(): member_total = lax.psum(local_error, 'mp')  5.77 us
  transfers between devices with their start and end apart: 2, of which 1 were waited for; matrix products, arithmetic and copies ran while one was open for 3% of the time, Pallas kernels for 0%

commit v1 on v0

--- a/solution.py
+++ b/solution.py
@@ -1,8 +1,11 @@
+import functools
 import math
 
 import jax
 import jax.numpy as jnp
 from jax import lax
+from jax.experimental import pallas as pl
+from jax.experimental.pallas import tpu as pltpu
 from jax.sharding import PartitionSpec as P
 
 SIGMA = 1.0
@@ -74,6 +77,368 @@
     return (update, fitness, stream)
 
 
+BLK = 256
+F32 = jnp.float32
+BF = jnp.bfloat16
+
+
+def nt_dot(a, b):
+    return lax.dot_general(a, b, (((1,), (1,)), ((), ())), preferred_element_type=F32)
+
+
+def split_two(x):
+    hi = x.astype(BF)
+    return hi, (x - hi.astype(F32)).astype(BF)
+
+
+def row_sums(ones, acc):
+    hi = acc.astype(BF)
+    rest = acc - hi.astype(F32)
+    mid, low = split_two(rest)
+    return nt_dot(ones, hi) + nt_dot(ones, mid) + nt_dot(ones, low)
+
+
+def fold_lanes(x):
+    total = x[:, :128]
+    for i in range(1, x.shape[1] // 128):
+        total = total + x[:, i * 128:(i + 1) * 128]
+    return total
+
+
+def kernel(
+    n_pop, n_mp, ctx_h, w_h, res_h, tgt_h, gain, left_h, right_h, right, ranks,
+    base, weighted, right_all, fit_out,
+    w_v, ctx, res, tgt, lcols, send_a, recv_a, send_y, recv_y, send_b, recv_b,
+    lall, rall, uall, mixed, sq_s, sq_a, sq_e, pre, pre_in, post, post_in, part_m, fits,
+    w_sem, loc_sem, sa, ra, sy, ry, sb, rb, s_pre, r_pre, s_post, r_post, s_m, r_m,
+    s_l, r_l, s_r, r_r, s_u, r_u, s_f, r_f,
+):
+    tok, width = ctx.shape
+    mem = right.shape[0]
+    full = right.shape[1]
+    rows = full // n_pop
+    chunks = width // BLK
+    quarter = tok // n_mp
+    members = mem * n_pop
+    p = lax.axis_index("pop")
+    q = lax.axis_index("mp")
+    y = q // 2
+    c = q % 2
+    mate = y * 2 + (1 - c)
+    across = (1 - y) * 2 + c
+    diagonal = (1 - y) * 2 + (1 - c)
+    blocks = (diagonal, across, mate, q)
+
+    def remote(src, dst, ss, rs, pop, mp):
+        return pltpu.make_async_remote_copy(
+            src_ref=src, dst_ref=dst, send_sem=ss, recv_sem=rs,
+            device_id=(pop, mp), device_id_type=pl.DeviceIdType.MESH,
+        )
+
+    def w_copy(s, k):
+        start = pl.multiple_of(blocks[s] * width + k * BLK, BLK)
+        return pltpu.make_async_copy(w_h.at[:, pl.ds(start, BLK)], w_v.at[s, k], w_sem.at[s, k])
+
+    my_cols = pl.ds(pl.multiple_of(q * width, BLK), width)
+    my_rows = pl.ds(pl.multiple_of(p * rows, 128), rows)
+    locals_ = [
+        pltpu.make_async_copy(ctx_h, ctx, loc_sem.at[0]),
+        pltpu.make_async_copy(res_h, res, loc_sem.at[1]),
+        pltpu.make_async_copy(tgt_h, tgt, loc_sem.at[2]),
+        pltpu.make_async_copy(left_h.at[:, my_cols], lcols, loc_sem.at[3]),
+        pltpu.make_async_copy(left_h.at[:, my_rows], lall.at[0], loc_sem.at[4]),
+        pltpu.make_async_copy(right_h.at[:, my_cols], rall.at[0], loc_sem.at[5]),
+    ]
+    locals_[0].start()
+    for k in range(chunks):
+        w_copy(0, k).start()
+        w_copy(1, k).start()
+    for k in range(chunks):
+        w_copy(2, k).start()
+        w_copy(3, k).start()
+    for item in locals_[1:]:
+        item.start()
+
+    barrier = pltpu.get_barrier_semaphore()
+    for d in range(1, n_mp):
+        pl.semaphore_signal(barrier, inc=1, device_id=(p, (q + d) % n_mp), device_id_type=pl.DeviceIdType.MESH)
+    for d in range(1, n_pop):
+        pl.semaphore_signal(barrier, inc=1, device_id=((p + d) % n_pop, q), device_id_type=pl.DeviceIdType.MESH)
+    pl.semaphore_wait(barrier, n_mp - 1 + n_pop - 1)
+
+    def copy_a(k):
+        return remote(send_a.at[k], recv_a.at[k], sa.at[k], ra.at[k], p, mate)
+
+    def copy_y(k):
+        return remote(send_y.at[k], recv_y.at[k], sy.at[k], ry.at[k], p, across)
+
+    def copy_b(k):
+        return remote(send_b.at[k], recv_b.at[k], sb.at[k], rb.at[k], p, mate)
+
+    def copy_l(d):
+        peer = (p + d) % n_pop
+        cols = pl.ds(pl.multiple_of(peer * rows, 128), rows)
+        return remote(left_h.at[:, cols], lall.at[d], s_l.at[d - 1], r_l.at[d - 1], peer, q)
+
+    def copy_r(d):
+        return remote(right_h.at[:, my_cols], rall.at[d], s_r.at[d - 1], r_r.at[d - 1], (p + d) % n_pop, q)
+
+    def copy_u(d):
+        return remote(ranks, uall.at[d], s_u.at[d - 1], r_u.at[d - 1], (p + d) % n_pop, q)
+
+    def copy_f(d):
+        return remote(fits.at[0], fits.at[d], s_f.at[d - 1], r_f.at[d - 1], (p + d) % n_pop, q)
+
+    def copy_pre(d):
+        peer = (q + d) % n_mp
+        return remote(pre.at[peer], pre_in.at[d - 1], s_pre.at[d - 1], r_pre.at[d - 1], p, peer)
+
+    def copy_post(d):
+        peer = (q + d) % n_mp
+        return remote(post.at[peer], post_in.at[d - 1], s_post.at[d - 1], r_post.at[d - 1], p, peer)
+
+    def copy_m(d):
+        return remote(part_m.at[q], part_m.at[q], s_m.at[d - 1], r_m.at[d - 1], p, (q + d) % n_mp)
+
+    def arrive_m(d):
+        source = (q + n_mp - d) % n_mp
+        return remote(part_m.at[source], part_m.at[source], s_m.at[d - 1], r_m.at[d - 1], p, source)
+
+    locals_[0].wait()
+
+    def far(k, carry):
+        w_copy(0, k).wait()
+        send_a[k] = jnp.dot(ctx[...], w_v[0, k], preferred_element_type=F32).astype(BF)
+        copy_a(k).start()
+        w_copy(1, k).wait()
+        mine = jnp.dot(ctx[...], w_v[1, k], preferred_element_type=F32)
+        copy_a(k).wait_recv()
+        send_y[k] = (mine + recv_a[k].astype(F32)).astype(BF)
+        copy_y(k).start()
+        return carry
+
+    lax.fori_loop(0, chunks, far, 0)
+
+    for d in range(1, n_pop):
+        copy_l(d).start()
+        copy_r(d).start()
+        copy_u(d).start()
+
+    for item in locals_[1:]:
+        item.wait()
+
+    def near(k, carry):
+        w_copy(2, k).wait()
+        send_b[k] = jnp.dot(ctx[...], w_v[2, k], preferred_element_type=F32).astype(BF)
+        copy_b(k).start()
+        w_copy(3, k).wait()
+        cols = pl.ds(pl.multiple_of(k * BLK, BLK), BLK)
+        base[:, cols] = jnp.dot(ctx[...], w_v[3, k], preferred_element_type=F32) + res[:, cols].astype(F32)
+        return carry
+
+    lax.fori_loop(0, chunks, near, 0)
+
+    ones = jnp.ones((8, 128), BF)
+    gain_mine = gain[:, my_cols]
+    r_mine = rall[0].astype(F32)
+    gr_hi, gr_lo = split_two(r_mine * gain_mine)
+    for t in range(n_mp):
+        part = slice(t * quarter, (t + 1) * quarter)
+        target = tgt[part, :]
+        pre[t, 0:mem, :] = nt_dot(lcols[...], ctx[part, :])
+        pre[t, mem:2 * mem, :] = nt_dot(gr_hi, target) + nt_dot(gr_lo, target)
+        wide = target.astype(F32)
+        pre[t, 2 * mem:2 * mem + 8, :] = row_sums(ones, fold_lanes(wide * wide))
+    for d in range(1, n_mp):
+        copy_pre(d).start()
+    g2_hi, g2_lo = split_two(r_mine * (gain_mine * gain_mine))
+    for k in range(chunks):
+        cols = slice(k * BLK, (k + 1) * BLK)
+        mixed[k, 0:mem, :] = rall[0, :, cols]
+        mixed[k, mem:2 * mem, :] = g2_hi[:, cols]
+        mixed[k, 2 * mem:3 * mem, :] = g2_lo[:, cols]
+    r_full = right[...].astype(F32)
+    gr_full = r_full * gain[...]
+    norm_r = jnp.sum(r_full * r_full, axis=1, keepdims=True)
+    norm_gr = jnp.sum(gr_full * gr_full, axis=1, keepdims=True)
+    sq_s[...] = jnp.zeros_like(sq_s)
+    sq_a[...] = jnp.zeros_like(sq_a)
+    sq_e[...] = jnp.zeros_like(sq_e)
+    post[...] = jnp.zeros_like(post)
+    uall[0] = ranks[...]
+
+    def settle(k, carry):
+        copy_b(k).wait_recv()
+        copy_y(k).wait_recv()
+        cols = pl.ds(pl.multiple_of(k * BLK, BLK), BLK)
+        gain_k = gain[:, pl.ds(pl.multiple_of(q * width + k * BLK, BLK), BLK)]
+        for t in range(n_mp):
+            part = slice(t * quarter, (t + 1) * quarter)
+            s = base[part, cols] + recv_b[k, part, :].astype(F32) + recv_y[k, part, :].astype(F32)
+            base[part, cols] = s
+            hi, low = split_two(s)
+            both = nt_dot(mixed[k], hi) + nt_dot(mixed[k], low)
+            post[t, 0:mem, :] += both[0:mem]
+            post[t, mem:2 * mem, :] += both[mem:2 * mem] + both[2 * mem:3 * mem]
+            gs = s * gain_k
+            sq_s[part, :] += fold_lanes(s * s)
+            sq_a[part, :] += fold_lanes(gs * gs)
+            sq_e[part, :] += fold_lanes(gs * tgt[part, cols].astype(F32))
+        return carry
+
+    lax.fori_loop(0, chunks, settle, 0)
+    for t in range(n_mp):
+        part = slice(t * quarter, (t + 1) * quarter)
+        post[t, 2 * mem:2 * mem + 8, :] = row_sums(ones, sq_s[part, :])
+        post[t, 2 * mem + 8:2 * mem + 16, :] = row_sums(ones, sq_a[part, :])
+        post[t, 2 * mem + 16:2 * mem + 24, :] = row_sums(ones, sq_e[part, :])
+    for d in range(1, n_mp):
+        copy_post(d).start()
+    early = pre[q]
+    for d in range(1, n_mp):
+        copy_pre(d).wait_recv()
+        early = early + pre_in[d - 1]
+    late = post[q]
+    for d in range(1, n_mp):
+        copy_post(d).wait_recv()
+        late = late + post_in[d - 1]
+    lifted = early[0:mem] * (SIGMA / math.sqrt(full))
+    cross_t = early[mem:2 * mem]
+    t_sq = early[2 * mem:2 * mem + 1]
+    crossed = late[0:mem]
+    crossed_g = late[mem:2 * mem]
+    s_sq = late[2 * mem:2 * mem + 1]
+    a_sq = late[2 * mem + 8:2 * mem + 9]
+    e_sq = late[2 * mem + 16:2 * mem + 17]
+    meansq = (s_sq + 2.0 * lifted * crossed + lifted * lifted * norm_r) / full
+    inverse = lax.rsqrt(meansq + EPSILON)
+    power = a_sq + 2.0 * lifted * crossed_g + lifted * lifted * norm_gr
+    errors = inverse * inverse * power - 2.0 * inverse * (e_sq + lifted * cross_t) + t_sq
+    part_m[q] = jnp.broadcast_to(jnp.sum(errors, axis=1, keepdims=True), (mem, 128))
+    for d in range(1, n_mp):
+        copy_m(d).start()
+    for d in range(1, n_mp):
+        arrive_m(d).wait_recv()
+    total = part_m[0]
+    for i in range(1, n_mp):
+        total = total + part_m[i]
+    fitness = -total / (tok * full)
+    fits[0] = fitness
+    for d in range(1, n_pop):
+        copy_f(d).start()
+    fit_out[...] = fitness
+    for d in range(1, n_pop):
+        copy_l(d).wait_recv()
+        copy_r(d).wait_recv()
+        copy_u(d).wait_recv()
+    right_all[...] = rall[...]
+    ceiling = math.log(members / 2 + 1)
+    whole = sum(max(0.0, ceiling - math.log(i + 1.0)) for i in range(members))
+    shaped = jnp.maximum(0.0, ceiling - jnp.log(uall[...] + 1.0)) / whole - 1.0 / members
+    for d in range(1, n_pop):
+        copy_f(d).wait_recv()
+    everyone = fits[...]
+    average = jnp.sum(jnp.sum(everyone, axis=0), axis=0, keepdims=True) / members
+    centre = everyone - average[None]
+    spread = jnp.sqrt(jnp.sum(jnp.sum(centre * centre, axis=0), axis=0, keepdims=True) / members + 1e-05)
+    weight = shaped + centre / spread[None] / members
+    for d in range(n_pop):
+        for i in range(rows // 128):
+            cols = slice(i * 128, (i + 1) * 128)
+            weighted[d, :, cols] = (weight[d] * lall[d, :, cols].astype(F32)).astype(BF)
+
+    def drain(k, carry):
+        copy_a(k).wait_send()
+        copy_y(k).wait_send()
+        copy_b(k).wait_send()
+        return carry
+
+    lax.fori_loop(0, chunks, drain, 0)
+    for d in range(1, n_mp):
+        copy_pre(d).wait_send()
+        copy_post(d).wait_send()
+        copy_m(d).wait_send()
+    for d in range(1, n_pop):
+        copy_l(d).wait_send()
+        copy_r(d).wait_send()
+        copy_u(d).wait_send()
+        copy_f(d).wait_send()
+
+
+def fused_shards(
+    n_pop, n_mp, context, out_weight, residual, target, norm_gain, left_factors, right_factors, member_ranks
+):
+    tok, width = context.shape
+    full = out_weight.shape[1]
+    mem = left_factors.shape[0]
+    rows = full // n_pop
+    chunks = width // BLK
+    quarter = tok // n_mp
+    ranks = jnp.broadcast_to(member_ranks.astype(F32)[:, None], (mem, 128))
+    anywhere = pl.BlockSpec(memory_space=pltpu.HBM)
+    vmem = pl.BlockSpec(memory_space=pltpu.VMEM)
+    block = pltpu.VMEM((chunks, tok, BLK), BF)
+    dma = pltpu.SemaphoreType.DMA
+    acc = pltpu.VMEM((tok, 128), F32)
+    base, weighted, right_all, fitness = pl.pallas_call(
+        functools.partial(kernel, n_pop, n_mp),
+        name="es_step",
+        out_shape=(
+            jax.ShapeDtypeStruct((tok, width), F32),
+            jax.ShapeDtypeStruct((n_pop, mem, rows), BF),
+            jax.ShapeDtypeStruct((n_pop, mem, width), BF),
+            jax.ShapeDtypeStruct((mem, 128), F32),
+        ),
+        in_specs=[anywhere] * 4 + [vmem, anywhere, anywhere, vmem, vmem],
+        out_specs=[vmem] * 4,
+        scratch_shapes=[
+            pltpu.VMEM((4, chunks, width, BLK), BF),
+            pltpu.VMEM((tok, width), BF),
+            pltpu.VMEM((tok, width), BF),
+            pltpu.VMEM((tok, width), BF),
+            pltpu.VMEM((mem, width), BF),
+            block, block, block, block, block, block,
+            pltpu.VMEM((n_pop, mem, rows), BF),
+            pltpu.VMEM((n_pop, mem, width), BF),
+            pltpu.VMEM((n_pop, mem, 128), F32),
+            pltpu.VMEM((chunks, 3 * mem, BLK), BF),
+            acc, acc, acc,
+            pltpu.VMEM((n_mp, 2 * mem + 8, quarter), F32),
+            pltpu.VMEM((n_mp - 1, 2 * mem + 8, quarter), F32),
+            pltpu.VMEM((n_mp, 2 * mem + 24, quarter), F32),
+            pltpu.VMEM((n_mp - 1, 2 * mem + 24, quarter), F32),
+            pltpu.VMEM((n_mp, mem, 128), F32),
+            pltpu.VMEM((n_pop, mem, 128), F32),
+            dma((4, chunks)),
+            dma((6,)),
+        ]
+        + [dma((chunks,))] * 6
+        + [dma((n_mp - 1,))] * 6
+        + [dma((n_pop - 1,))] * 8,
+        compiler_params=pltpu.CompilerParams(
+            collective_id=0, has_side_effects=True, vmem_limit_bytes=48 * 1024 * 1024
+        ),
+    )(
+        context, out_weight, residual, target, norm_gain.reshape(1, full), left_factors,
+        right_factors, right_factors, ranks,
+    )
+    count_all = n_pop * mem
+    update = lax.dot_general(
+        weighted.reshape(count_all, rows), right_all.reshape(count_all, width),
+        (((0,), (0,)), ((), ())), preferred_element_type=F32,
+    ) * (math.sqrt(count_all) / SIGMA)
+    return (update, fitness[:, 0], base)
+
+
+def chosen(n_pop, n_mp, context, out_weight, *rest):
+    tok, width = context.shape
+    mem = rest[3].shape[0]
+    full = out_weight.shape[1]
+    if n_mp == 4 and width % BLK == 0 and (full // n_pop) % 128 == 0 and tok % (16 * n_mp) == 0 and mem % 16 == 0:
+        return fused_shards(n_pop, n_mp, context, out_weight, *rest)
+    return shards(context, out_weight, *rest)
+
+
 def solution(mesh):
     in_specs = (
         P("pop", "mp"),
@@ -86,4 +451,5 @@
         P("pop"),
     )
     out_specs = (P("pop", "mp"), P("pop"), P("pop", "mp"))
-    return jax.shard_map(shards, mesh=mesh, in_specs=in_specs, out_specs=out_specs, check_vma=False)
+    return jax.shard_map(
+        functools.partial(chosen, mesh.shape["pop"], mesh.shape["mp"]), mesh=mesh, in_specs=in_specs, out_specs=out_specs, check_vma=False)

time: 170 us -> 55.7 us (0.33)
  blocking collectives: 69.9 us -> 0 us
  Pallas kernels: 0 us -> 43.6 us
  waiting for transfers between devices: 39.6 us -> 0 us
  other arithmetic: 20.5 us -> 0.66 us
  between operations: 16.1 us -> 0.65 us
  matrix products: 15.9 us -> 2.33 us
  local copies, waits for them, and re-layouts: 3.75 us -> 8.13 us
  starting transfers between devices: 3.42 us -> 0 us
    pallas_call x0 -> x1, Pallas kernels: none -> 43.6 us  [fused_shards(): pl.pallas_call(functools.partial(kernel, n_pop, n_mp), name='es_step', ou...]
    reduce_scatter x1 -> x0, waiting for transfers between devices: 39.6 us -> none  [shards(): lax.psum_scatter(partial_value.astype(jnp.bfloat16), 'mp', scatter_dimens...]
    all_gather x1 -> x0, blocking collectives: 31.9 us -> none  [shards(): right_all = lax.all_gather(right_cols, 'pop', axis=0, tiled=True)]
    unnamed x1 -> x0, blocking collectives: 21.5 us -> none
    reduce_sum x6 -> x0, other arithmetic: 16.6 us -> none  [the longest x1 12.8 us: error_sums(): return jnp.sum(differ * differ, axis=(0, 2))]
    psum x2 -> x0, blocking collectives: 16.5 us -> none  [the longest x1 10.7 us: shards(): lax.psum((projected, crossed, per_token, per_member), 'mp')]
    dot_general x4 -> x1, matrix products: 15.9 us -> 2.33 us  [fused_shards(): lax.dot_general(weighted.reshape(count_all, rows), right_all.reshape(coun...]
    unnamed x13, local copies, waits for them, and re-layouts: 2.04 us -> 7.43 us
  transfers between devices with their start and end apart: 2 -> 0, of which waited for: 1 -> 0; matrix products, arithmetic and copies ran while one was open for 3% -> 0% of each run, Pallas kernels for 0% -> 0%
where the time goes in v1:
time: 55.7 us; the launch traced here: 55.4 us
  Pallas kernels  43.6 us (78%)
  local copies, waits for them, and re-layouts  8.13 us (15%)
  matrix products  2.33 us (4%)
  other arithmetic  0.66 us (1%)
  between operations  0.65 us (1%)
    pallas_call x1, Pallas kernels, fused_shards(): pl.pallas_call(functools.partial(kernel, n_pop, n_mp), name='es_step', ou...  43.6 us
    unnamed x13, local copies, waits for them, and re-layouts  7.43 us
    dot_general x1, matrix products, fused_shards(): lax.dot_general(weighted.reshape(count_all, rows), right_all.reshape(coun...  2.33 us

profile of v1, /device:TPU:0, one launch (start us, length us, event | category | flops | bytes accessed | tf_op | source)
XLA Modules:
  0.0 55.4 jit_solution(10070651885292874711)
XLA Ops:
  0.6 0.7 %convert_element_type.3 = f32[16]{0:T(128)S(1)} convert(s32[16]{0:T(128)} %param.15) | non-fusion elementwise | flops 16 | bytes 128 | tf_op jit(solution)/shard_map/convert_element_type | solution.py:377
  1.3 0.1 broadcast_in_dim.2.ranks
  1.4 0.0 copy-start
  1.4 1.2 %copy-done = bf16[384,1280]{1,0:T(8,128)(2,1)S(1)} copy-done((bf16[384,1280]{1,0:T(8,128)(2,1)S(1)}, bf16[384,1280]{1,0:T(8,128)(2,1)}, u32[]{:S(2)}) %copy-start) | copy-done | bytes 983064
  2.6 0.0 copy-start.1
  2.6 1.2 %copy-done.1 = bf16[384,1280]{1,0:T(8,128)(2,1)S(1)} copy-done((bf16[384,1280]{1,0:T(8,128)(2,1)S(1)}, bf16[384,1280]{1,0:T(8,128)(2,1)}, u32[]{:S(2)}) %copy-start.1) | copy-done | bytes 983064
  3.8 0.0 copy-start.2
  3.8 1.2 %copy-done.2 = bf16[384,1280]{1,0:T(8,128)(2,1)S(1)} copy-done((bf16[384,1280]{1,0:T(8,128)(2,1)S(1)}, bf16[384,1280]{1,0:T(8,128)(2,1)}, u32[]{:S(2)}) %copy-start.2) | copy-done | bytes 983064
  5.0 0.0 copy-start.3
  5.0 0.9 %copy-done.3 = bf16[16,5120]{1,0:T(8,128)(2,1)S(1)} copy-done((bf16[16,5120]{1,0:T(8,128)(2,1)S(1)}, bf16[16,5120]{1,0:T(8,128)(2,1)}, u32[]{:S(2)}) %copy-start.3) | copy-done | bytes 163864
  5.9 0.0 copy-start.4
  5.9 0.9 %copy-done.4 = bf16[16,5120]{1,0:T(8,128)(2,1)S(1)} copy-done((bf16[16,5120]{1,0:T(8,128)(2,1)S(1)}, bf16[16,5120]{1,0:T(8,128)(2,1)}, u32[]{:S(2)}) %copy-start.4) | copy-done | bytes 163864
  6.8 0.0 copy-start.5
  6.8 0.7 %copy-done.5 = f32[5120]{0:T(1024)S(1)} copy-done((f32[5120]{0:T(1024)S(1)}, f32[5120]{0:T(1024)}, u32[]{:S(2)}) %copy-start.5) | copy-done | bytes 20504
  7.5 43.6 %es_step.1 = (f32[384,1280]{1,0:T(8,128)S(1)}, bf16[8,16,640]{2,1,0:T(8,128)(2,1)S(1)}, bf16[8,16,1280]{2,1,0:T(8,128)(2,1)S(1)}, f32[16,128]{1,0:T(8,128)S(1)}) custom-call(bf16[384,1280]{1,0:T(8,128)(2,1)S(1)} %copy-done, bf16[1280,5120]{1,0:T(8,128)(2,1)} %w_h.1, bf16[384,1280]{1,0:T(8,128)(2,1)S(1)} %copy-done.1, bf16[384,1280]{1,0:T(8,128)(2,1)S(1)} %copy-done.2, ...), custom_call_target="tpu_custom_call" | custom-call | tf_op jit(solution)/shard_map/es_step/pallas_call | solution.py:383
  51.1 0.6 %slice_reduce_fusion = f32[16]{0:T(128)} fusion(f32[16,128]{1,0:T(8,128)S(1)} %get-tuple-element.9), kind=kLoop, calls=%fused_computation.2 | loop fusion | bytes 128 | tf_op jit(solution)/shard_map/slice | solution.py:430
  51.8 2.3 %fusion = f32[640,1280]{1,0:T(8,128)} fusion(bf16[8,16,640]{2,1,0:T(8,128)(2,1)S(1)} %get-tuple-element.7, bf16[8,16,1280]{2,1,0:T(8,128)(2,1)S(1)} %get-tuple-element.8), kind=kOutput, calls=%fused_computation.1 | convolution fusion | flops 210534400 | bytes 3768320 | tf_op jit(solution)/shard_map/dot_general | solution.py:426
  54.1 1.3 %copy.12 = f32[384,1280]{1,0:T(8,128)} copy(f32[384,1280]{1,0:T(8,128)S(1)} %get-tuple-element.16) | data formatting | bytes 3932160
Async XLA Ops:
  1.4 1.2 %copy-start = (bf16[384,1280]{1,0:T(8,128)(2,1)S(1)}, bf16[384,1280]{1,0:T(8,128)(2,1)}, u32[]{:S(2)}) copy-start(bf16[384,1280]{1,0:T(8,128)(2,1)} %ctx_h.1) | copy-start | bytes 2949124
  2.6 1.2 %copy-start.1 = (bf16[384,1280]{1,0:T(8,128)(2,1)S(1)}, bf16[384,1280]{1,0:T(8,128)(2,1)}, u32[]{:S(2)}) copy-start(bf16[384,1280]{1,0:T(8,128)(2,1)} %res_h.1) | copy-start | bytes 2949124
  3.8 1.2 %copy-start.2 = (bf16[384,1280]{1,0:T(8,128)(2,1)S(1)}, bf16[384,1280]{1,0:T(8,128)(2,1)}, u32[]{:S(2)}) copy-start(bf16[384,1280]{1,0:T(8,128)(2,1)} %tgt_h.1) | copy-start | bytes 2949124
  5.0 0.9 %copy-start.3 = (bf16[16,5120]{1,0:T(8,128)(2,1)S(1)}, bf16[16,5120]{1,0:T(8,128)(2,1)}, u32[]{:S(2)}) copy-start(bf16[16,5120]{1,0:T(8,128)(2,1)} %right.1) | copy-start | bytes 491524
  5.9 0.9 %copy-start.4 = (bf16[16,5120]{1,0:T(8,128)(2,1)S(1)}, bf16[16,5120]{1,0:T(8,128)(2,1)}, u32[]{:S(2)}) copy-start(bf16[16,5120]{1,0:T(8,128)(2,1)} %left_h.1) | copy-start | bytes 491524
  6.8 0.7 %copy-start.5 = (f32[5120]{0:T(1024)S(1)}, f32[5120]{0:T(1024)}, u32[]{:S(2)}) copy-start(f32[5120]{0:T(1024)} %param.12) | copy-start | bytes 61444

commit v2 on v1

--- a/solution.py
+++ b/solution.py
@@ -151,10 +151,9 @@
     ]
     locals_[0].start()
     for k in range(chunks):
-        w_copy(0, k).start()
-        w_copy(1, k).start()
+        for s in range(3):
+            w_copy(s, k).start()
     for k in range(chunks):
-        w_copy(2, k).start()
         w_copy(3, k).start()
     for item in locals_[1:]:
         item.start()
@@ -184,7 +183,7 @@
         return remote(right_h.at[:, my_cols], rall.at[d], s_r.at[d - 1], r_r.at[d - 1], (p + d) % n_pop, q)
 
     def copy_u(d):
-        return remote(ranks, uall.at[d], s_u.at[d - 1], r_u.at[d - 1], (p + d) % n_pop, q)
+        return remote(uall.at[0], uall.at[d], s_u.at[d - 1], r_u.at[d - 1], (p + d) % n_pop, q)
 
     def copy_f(d):
         return remote(fits.at[0], fits.at[d], s_f.at[d - 1], r_f.at[d - 1], (p + d) % n_pop, q)
@@ -212,6 +211,9 @@
         copy_a(k).start()
         w_copy(1, k).wait()
         mine = jnp.dot(ctx[...], w_v[1, k], preferred_element_type=F32)
+        w_copy(2, k).wait()
+        send_b[k] = jnp.dot(ctx[...], w_v[2, k], preferred_element_type=F32).astype(BF)
+        copy_b(k).start()
         copy_a(k).wait_recv()
         send_y[k] = (mine + recv_a[k].astype(F32)).astype(BF)
         copy_y(k).start()
@@ -219,6 +221,7 @@
 
     lax.fori_loop(0, chunks, far, 0)
 
+    uall[0] = ranks[...].astype(F32)
     for d in range(1, n_pop):
         copy_l(d).start()
         copy_r(d).start()
@@ -228,9 +231,6 @@
         item.wait()
 
     def near(k, carry):
-        w_copy(2, k).wait()
-        send_b[k] = jnp.dot(ctx[...], w_v[2, k], preferred_element_type=F32).astype(BF)
-        copy_b(k).start()
         w_copy(3, k).wait()
         cols = pl.ds(pl.multiple_of(k * BLK, BLK), BLK)
         base[:, cols] = jnp.dot(ctx[...], w_v[3, k], preferred_element_type=F32) + res[:, cols].astype(F32)
@@ -265,7 +265,6 @@
     sq_a[...] = jnp.zeros_like(sq_a)
     sq_e[...] = jnp.zeros_like(sq_e)
     post[...] = jnp.zeros_like(post)
-    uall[0] = ranks[...]
 
     def settle(k, carry):
         copy_b(k).wait_recv()
@@ -287,11 +286,11 @@
         return carry
 
     lax.fori_loop(0, chunks, settle, 0)
+    line = lax.broadcasted_iota(jnp.int32, (8, quarter), 0)
     for t in range(n_mp):
         part = slice(t * quarter, (t + 1) * quarter)
-        post[t, 2 * mem:2 * mem + 8, :] = row_sums(ones, sq_s[part, :])
-        post[t, 2 * mem + 8:2 * mem + 16, :] = row_sums(ones, sq_a[part, :])
-        post[t, 2 * mem + 16:2 * mem + 24, :] = row_sums(ones, sq_e[part, :])
+        rest = jnp.where(line == 1, row_sums(ones, sq_a[part, :]), row_sums(ones, sq_e[part, :]))
+        post[t, 2 * mem:2 * mem + 8, :] = jnp.where(line == 0, row_sums(ones, sq_s[part, :]), rest)
     for d in range(1, n_mp):
         copy_post(d).start()
     early = pre[q]
@@ -308,13 +307,13 @@
     crossed = late[0:mem]
     crossed_g = late[mem:2 * mem]
     s_sq = late[2 * mem:2 * mem + 1]
-    a_sq = late[2 * mem + 8:2 * mem + 9]
-    e_sq = late[2 * mem + 16:2 * mem + 17]
+    a_sq = late[2 * mem + 1:2 * mem + 2]
+    e_sq = late[2 * mem + 2:2 * mem + 3]
     meansq = (s_sq + 2.0 * lifted * crossed + lifted * lifted * norm_r) / full
     inverse = lax.rsqrt(meansq + EPSILON)
     power = a_sq + 2.0 * lifted * crossed_g + lifted * lifted * norm_gr
     errors = inverse * inverse * power - 2.0 * inverse * (e_sq + lifted * cross_t) + t_sq
-    part_m[q] = jnp.broadcast_to(jnp.sum(errors, axis=1, keepdims=True), (mem, 128))
+    part_m[q] = row_sums(jnp.ones((8, quarter), BF), errors)[0:1]
     for d in range(1, n_mp):
         copy_m(d).start()
     for d in range(1, n_mp):
@@ -331,21 +330,23 @@
         copy_l(d).wait_recv()
         copy_r(d).wait_recv()
         copy_u(d).wait_recv()
-    right_all[...] = rall[...]
+    for d in range(n_pop):
+        right_all[d * mem:(d + 1) * mem, :] = rall[d]
     ceiling = math.log(members / 2 + 1)
     whole = sum(max(0.0, ceiling - math.log(i + 1.0)) for i in range(members))
     shaped = jnp.maximum(0.0, ceiling - jnp.log(uall[...] + 1.0)) / whole - 1.0 / members
     for d in range(1, n_pop):
         copy_f(d).wait_recv()
     everyone = fits[...]
-    average = jnp.sum(jnp.sum(everyone, axis=0), axis=0, keepdims=True) / members
+    average = jnp.sum(jnp.sum(everyone, axis=0), axis=1, keepdims=True) / members
     centre = everyone - average[None]
-    spread = jnp.sqrt(jnp.sum(jnp.sum(centre * centre, axis=0), axis=0, keepdims=True) / members + 1e-05)
+    spread = jnp.sqrt(jnp.sum(jnp.sum(centre * centre, axis=0), axis=1, keepdims=True) / members + 1e-05)
     weight = shaped + centre / spread[None] / members
+    square = (mem, mem)
+    eye = lax.broadcasted_iota(jnp.int32, square, 0) == lax.broadcasted_iota(jnp.int32, square, 1)
     for d in range(n_pop):
-        for i in range(rows // 128):
-            cols = slice(i * 128, (i + 1) * 128)
-            weighted[d, :, cols] = (weight[d] * lall[d, :, cols].astype(F32)).astype(BF)
+        upright = jnp.sum(jnp.where(eye, weight[d], 0.0), axis=1, keepdims=True)
+        weighted[d * mem:(d + 1) * mem, :] = (upright * lall[d].astype(F32)).astype(BF)
 
     def drain(k, carry):
         copy_a(k).wait_send()
@@ -363,6 +364,10 @@
         copy_r(d).wait_send()
         copy_u(d).wait_send()
         copy_f(d).wait_send()
+
+
+def in_hbm(x):
+    return pltpu.with_memory_space_constraint(x, pltpu.HBM)
 
 
 def fused_shards(
@@ -374,7 +379,7 @@
     rows = full // n_pop
     chunks = width // BLK
     quarter = tok // n_mp
-    ranks = jnp.broadcast_to(member_ranks.astype(F32)[:, None], (mem, 128))
+    ranks = member_ranks.reshape(1, mem)
     anywhere = pl.BlockSpec(memory_space=pltpu.HBM)
     vmem = pl.BlockSpec(memory_space=pltpu.VMEM)
     block = pltpu.VMEM((chunks, tok, BLK), BF)
@@ -385,9 +390,9 @@
         name="es_step",
         out_shape=(
             jax.ShapeDtypeStruct((tok, width), F32),
-            jax.ShapeDtypeStruct((n_pop, mem, rows), BF),
-            jax.ShapeDtypeStruct((n_pop, mem, width), BF),
-            jax.ShapeDtypeStruct((mem, 128), F32),
+            jax.ShapeDtypeStruct((n_pop * mem, rows), BF),
+            jax.ShapeDtypeStruct((n_pop * mem, width), BF),
+            jax.ShapeDtypeStruct((1, mem), F32),
         ),
         in_specs=[anywhere] * 4 + [vmem, anywhere, anywhere, vmem, vmem],
         out_specs=[vmem] * 4,
@@ -400,15 +405,15 @@
             block, block, block, block, block, block,
             pltpu.VMEM((n_pop, mem, rows), BF),
             pltpu.VMEM((n_pop, mem, width), BF),
-            pltpu.VMEM((n_pop, mem, 128), F32),
+            pltpu.VMEM((n_pop, 1, mem), F32),
             pltpu.VMEM((chunks, 3 * mem, BLK), BF),
             acc, acc, acc,
             pltpu.VMEM((n_mp, 2 * mem + 8, quarter), F32),
             pltpu.VMEM((n_mp - 1, 2 * mem + 8, quarter), F32),
-            pltpu.VMEM((n_mp, 2 * mem + 24, quarter), F32),
-            pltpu.VMEM((n_mp - 1, 2 * mem + 24, quarter), F32),
-            pltpu.VMEM((n_mp, mem, 128), F32),
-            pltpu.VMEM((n_pop, mem, 128), F32),
+            pltpu.VMEM((n_mp, 2 * mem + 8, quarter), F32),
+            pltpu.VMEM((n_mp - 1, 2 * mem + 8, quarter), F32),
+            pltpu.VMEM((n_mp, 1, mem), F32),
+            pltpu.VMEM((n_pop, 1, mem), F32),
             dma((4, chunks)),
             dma((6,)),
         ]
@@ -419,22 +424,51 @@
             collective_id=0, has_side_effects=True, vmem_limit_bytes=48 * 1024 * 1024
         ),
     )(
-        context, out_weight, residual, target, norm_gain.reshape(1, full), left_factors,
-        right_factors, right_factors, ranks,
+        *map(in_hbm, (context, out_weight, residual, target)), norm_gain.reshape(1, full),
+        in_hbm(left_factors), in_hbm(right_factors), right_factors, ranks,
     )
     count_all = n_pop * mem
-    update = lax.dot_general(
-        weighted.reshape(count_all, rows), right_all.reshape(count_all, width),
-        (((0,), (0,)), ((), ())), preferred_element_type=F32,
-    ) * (math.sqrt(count_all) / SIGMA)
-    return (update, fitness[:, 0], base)
+    steps = rows // 128
+    part = width // steps
+    update, base, fitness = pl.pallas_call(
+        functools.partial(finish, math.sqrt(count_all) / SIGMA),
+        name="es_update",
+        grid=(steps,),
+        out_shape=(
+            jax.ShapeDtypeStruct((rows, width), F32),
+            jax.ShapeDtypeStruct((tok, width), F32),
+            jax.ShapeDtypeStruct((1, mem), F32),
+        ),
+        in_specs=[
+            pl.BlockSpec((count_all, 128), lambda i: (0, i)),
+            pl.BlockSpec((count_all, width), lambda i: (0, 0)),
+            pl.BlockSpec((tok, part), lambda i: (0, i)),
+            pl.BlockSpec((1, mem), lambda i: (0, 0)),
+        ],
+        out_specs=(
+            pl.BlockSpec((128, width), lambda i: (i, 0)),
+            pl.BlockSpec((tok, part), lambda i: (0, i)),
+            pl.BlockSpec((1, mem), lambda i: (0, 0)),
+        ),
+        compiler_params=pltpu.CompilerParams(vmem_limit_bytes=16 * 1024 * 1024),
+    )(weighted, right_all, base, fitness)
+    return (update, fitness.reshape(mem), base)
+
+
+def finish(scale, weighted, right_all, base_in, fit_in, update, base, fit):
+    update[...] = lax.dot_general(
+        weighted[...], right_all[...], (((0,), (0,)), ((), ())), preferred_element_type=F32
+    ) * scale
+    base[...] = base_in[...]
+    fit[...] = fit_in[...]
 
 
 def chosen(n_pop, n_mp, context, out_weight, *rest):
     tok, width = context.shape
     mem = rest[3].shape[0]
     full = out_weight.shape[1]
-    if n_mp == 4 and width % BLK == 0 and (full // n_pop) % 128 == 0 and tok % (16 * n_mp) == 0 and mem % 16 == 0:
+    full_rows = full // n_pop
+    if n_mp == 4 and width % BLK == 0 and (full // n_pop) % 128 == 0 and tok % (16 * n_mp) == 0 and mem % 16 == 0 and width % full_rows == 0:
         return fused_shards(n_pop, n_mp, context, out_weight, *rest)
     return shards(context, out_weight, *rest)
 

time: 55.7 us -> 52.4 us (0.941)
  local copies, waits for them, and re-layouts: 8.13 us -> 1.38 us
  Pallas kernels: 43.6 us -> 50.2 us
  matrix products: 2.33 us -> 0 us
  other arithmetic: 0.66 us -> 0 us
    unnamed x13 -> x4, local copies, waits for them, and re-layouts: 7.43 us -> 1.38 us
    pallas_call x0 -> x1, Pallas kernels: none -> 3.76 us  [fused_shards(): pl.pallas_call(functools.partial(finish, math.sqrt(count_all) / SIGMA), n...]
    pallas_call x1, Pallas kernels: 43.6 us -> 46.5 us  [fused_shards(): pl.pallas_call(functools.partial(kernel, n_pop, n_mp), name='es_step', ou...]
    dot_general x1 -> x0, matrix products: 2.33 us -> none  [fused_shards(): lax.dot_general(weighted.reshape(count_all, rows), right_all.reshape(coun...]
    convert_element_type x1 -> x0, other arithmetic: 0.66 us -> none  [fused_shards(): ranks = jnp.broadcast_to(member_ranks.astype(F32)[:, None], (mem, 128))]
    slice x1 -> x0, local copies, waits for them, and re-layouts: 0.63 us -> none  [fused_shards(): return (update, fitness[:, 0], base)]
where the time goes in v2:
time: 52.4 us; the launch traced here: 52.2 us
  Pallas kernels  50.2 us (96%)
  local copies, waits for them, and re-layouts  1.38 us (3%)
  between operations  0.65 us (1%)
    pallas_call x1, Pallas kernels, fused_shards(): pl.pallas_call(functools.partial(kernel, n_pop, n_mp), name='es_step', ou...  46.5 us
    pallas_call x1, Pallas kernels, fused_shards(): pl.pallas_call(functools.partial(finish, math.sqrt(count_all) / SIGMA), n...  3.76 us
    unnamed x4, local copies, waits for them, and re-layouts  1.38 us

profile of v2, /device:TPU:0, one launch (start us, length us, event | category | flops | bytes accessed | tf_op | source)
XLA Modules:
  0.0 52.2 jit_solution(771027319787390311)
XLA Ops:
  0.6 0.0 copy-start
  0.6 0.7 %copy-done = f32[5120]{0:T(1024)S(1)} copy-done((f32[5120]{0:T(1024)S(1)}, f32[5120]{0:T(1024)}, u32[]{:S(2)}) %copy-start) | copy-done | bytes 20504
  1.4 0.0 copy-start.1
  1.4 0.7 %copy-done.1 = s32[16]{0:T(128)S(1)} copy-done((s32[16]{0:T(128)S(1)}, s32[16]{0:T(128)}, u32[]{:S(2)}) %copy-start.1) | copy-done | bytes 88
  2.0 46.5 %es_step.1 = (f32[384,1280]{1,0:T(8,128)S(1)}, bf16[128,640]{1,0:T(8,128)(2,1)S(1)}, bf16[128,1280]{1,0:T(8,128)(2,1)S(1)}, f32[1,16]{1,0:T(1,128)S(1)}) custom-call(bf16[384,1280]{1,0:T(8,128)(2,1)} %ctx_h.1, bf16[1280,5120]{1,0:T(8,128)(2,1)} %w_h.1, bf16[384,1280]{1,0:T(8,128)(2,1)} %res_h.1, bf16[384,1280]{1,0:T(8,128)(2,1)} %tgt_h.1, ...), custom_call_target="tpu_custom_call" | custom-call | tf_op jit(solution)/shard_map/es_step/pallas_call | solution.py:388
  48.5 3.8 %es_update.1 = (f32[640,1280]{1,0:T(8,128)}, f32[384,1280]{1,0:T(8,128)}, f32[1,16]{1,0:T(1,128)}) custom-call(bf16[128,640]{1,0:T(8,128)(2,1)S(1)} %get-tuple-element.10.weighted, bf16[128,1280]{1,0:T(8,128)(2,1)S(1)} %get-tuple-element.11.right_all, f32[384,1280]{1,0:T(8,128)S(1)} %get-tuple-element.12.base_in, f32[1,16]{1,0:T(1,128)S(1)} %get-tuple-element.13.fit_in), custom_call_target="tpu_custom_call" | custom-call | tf_op jit(solution)/shard_map/es_update/pallas_call | solution.py:433
Async XLA Ops:
  0.6 0.7 %copy-start = (f32[5120]{0:T(1024)S(1)}, f32[5120]{0:T(1024)}, u32[]{:S(2)}) copy-start(f32[5120]{0:T(1024)} %param.12) | copy-start | bytes 61444
  1.4 0.7 %copy-start.1 = (s32[16]{0:T(128)S(1)}, s32[16]{0:T(128)}, u32[]{:S(2)}) copy-start(s32[16]{0:T(128)} %param.15) | copy-start | bytes 196

commit v3 on v2

--- a/solution.py
+++ b/solution.py
@@ -106,11 +106,11 @@
 
 
 def kernel(
-    n_pop, n_mp, ctx_h, w_h, res_h, tgt_h, gain, left_h, right_h, right, ranks,
+    n_pop, n_mp, ctx_h, w_h, res_h, tgt_h, gain_h, left_h, right_h, ranks_h,
     base, weighted, right_all, fit_out,
-    w_v, ctx, res, tgt, lcols, send_a, recv_a, send_y, recv_y, send_b, recv_b,
-    lall, rall, uall, mixed, sq_s, sq_a, sq_e, pre, pre_in, post, post_in, part_m, fits,
-    w_sem, loc_sem, sa, ra, sy, ry, sb, rb, s_pre, r_pre, s_post, r_post, s_m, r_m,
+    w_v, ctx, res, tgt, lcols, gain, right, ranks, send_a, recv_a, send_y, recv_y, send_b, recv_b,
+    lall, rall, uall, mixed, sq_s, sq_a, sq_e, pre, pre_in, post, post_in, fits,
+    w_sem, loc_sem, sa, ra, sy, ry, sb, rb, s_pre, r_pre, s_post, r_post,
     s_l, r_l, s_r, r_r, s_u, r_u, s_f, r_f,
 ):
     tok, width = ctx.shape
@@ -148,22 +148,21 @@
         pltpu.make_async_copy(left_h.at[:, my_cols], lcols, loc_sem.at[3]),
         pltpu.make_async_copy(left_h.at[:, my_rows], lall.at[0], loc_sem.at[4]),
         pltpu.make_async_copy(right_h.at[:, my_cols], rall.at[0], loc_sem.at[5]),
+        pltpu.make_async_copy(gain_h, gain, loc_sem.at[6]),
+        pltpu.make_async_copy(right_h, right, loc_sem.at[7]),
+        pltpu.make_async_copy(ranks_h, ranks, loc_sem.at[8]),
     ]
     locals_[0].start()
-    for k in range(chunks):
+    for k in range(2):
         for s in range(3):
             w_copy(s, k).start()
-    for k in range(chunks):
-        w_copy(3, k).start()
-    for item in locals_[1:]:
-        item.start()
 
     barrier = pltpu.get_barrier_semaphore()
-    for d in range(1, n_mp):
-        pl.semaphore_signal(barrier, inc=1, device_id=(p, (q + d) % n_mp), device_id_type=pl.DeviceIdType.MESH)
-    for d in range(1, n_pop):
-        pl.semaphore_signal(barrier, inc=1, device_id=((p + d) % n_pop, q), device_id_type=pl.DeviceIdType.MESH)
-    pl.semaphore_wait(barrier, n_mp - 1 + n_pop - 1)
+    peers = [(i, j) for i in range(n_pop) for j in range(n_mp)][1:]
+    for i, j in peers:
+        pl.semaphore_signal(
+            barrier, inc=1, device_id=((p + i) % n_pop, (q + j) % n_mp), device_id_type=pl.DeviceIdType.MESH
+        )
 
     def copy_a(k):
         return remote(send_a.at[k], recv_a.at[k], sa.at[k], ra.at[k], p, mate)
@@ -185,8 +184,14 @@
     def copy_u(d):
         return remote(uall.at[0], uall.at[d], s_u.at[d - 1], r_u.at[d - 1], (p + d) % n_pop, q)
 
-    def copy_f(d):
-        return remote(fits.at[0], fits.at[d], s_f.at[d - 1], r_f.at[d - 1], (p + d) % n_pop, q)
+    def copy_f(i, j):
+        n = i * n_mp + j - 1
+        return remote(fits.at[0, q], fits.at[i, q], s_f.at[n], r_f.at[n], (p + i) % n_pop, (q + j) % n_mp)
+
+    def arrive_f(i, j):
+        n = i * n_mp + j - 1
+        source = (q + n_mp - j) % n_mp
+        return remote(fits.at[i, source], fits.at[i, source], s_f.at[n], r_f.at[n], (p + n_pop - i) % n_pop, source)
 
     def copy_pre(d):
         peer = (q + d) % n_mp
@@ -196,44 +201,55 @@
         peer = (q + d) % n_mp
         return remote(post.at[peer], post_in.at[d - 1], s_post.at[d - 1], r_post.at[d - 1], p, peer)
 
-    def copy_m(d):
-        return remote(part_m.at[q], part_m.at[q], s_m.at[d - 1], r_m.at[d - 1], p, (q + d) % n_mp)
-
-    def arrive_m(d):
-        source = (q + n_mp - d) % n_mp
-        return remote(part_m.at[source], part_m.at[source], s_m.at[d - 1], r_m.at[d - 1], p, source)
+    def product(s, k):
+        w_copy(s, k).wait()
+        return jnp.dot(ctx[...], w_v[s, k], preferred_element_type=F32)
 
     locals_[0].wait()
+    send_a[0] = product(0, 0).astype(BF)
+    pl.semaphore_wait(barrier, n_mp * n_pop - 1)
+    copy_a(0).start()
 
     def far(k, carry):
-        w_copy(0, k).wait()
-        send_a[k] = jnp.dot(ctx[...], w_v[0, k], preferred_element_type=F32).astype(BF)
-        copy_a(k).start()
-        w_copy(1, k).wait()
-        mine = jnp.dot(ctx[...], w_v[1, k], preferred_element_type=F32)
-        w_copy(2, k).wait()
-        send_b[k] = jnp.dot(ctx[...], w_v[2, k], preferred_element_type=F32).astype(BF)
-        copy_b(k).start()
+        @pl.when(k + 2 < chunks)
+        def _():
+            for s in range(3):
+                w_copy(s, k + 2).start()
+
+        w_copy(3, k).start()
+
+        @pl.when(k == 1)
+        def _():
+            for item in locals_[1:]:
+                item.start()
+
+        mine = product(1, k)
+
+        @pl.when(k + 1 < chunks)
+        def _():
+            send_a[k + 1] = product(0, k + 1).astype(BF)
+            copy_a(k + 1).start()
+
         copy_a(k).wait_recv()
         send_y[k] = (mine + recv_a[k].astype(F32)).astype(BF)
         copy_y(k).start()
+        send_b[k] = product(2, k).astype(BF)
+        copy_b(k).start()
         return carry
 
     lax.fori_loop(0, chunks, far, 0)
 
+    for item in locals_[1:]:
+        item.wait()
     uall[0] = ranks[...].astype(F32)
     for d in range(1, n_pop):
         copy_l(d).start()
         copy_r(d).start()
         copy_u(d).start()
 
-    for item in locals_[1:]:
-        item.wait()
-
     def near(k, carry):
-        w_copy(3, k).wait()
         cols = pl.ds(pl.multiple_of(k * BLK, BLK), BLK)
-        base[:, cols] = jnp.dot(ctx[...], w_v[3, k], preferred_element_type=F32) + res[:, cols].astype(F32)
+        base[:, cols] = product(3, k) + res[:, cols].astype(F32)
         return carry
 
     lax.fori_loop(0, chunks, near, 0)
@@ -313,19 +329,9 @@
     inverse = lax.rsqrt(meansq + EPSILON)
     power = a_sq + 2.0 * lifted * crossed_g + lifted * lifted * norm_gr
     errors = inverse * inverse * power - 2.0 * inverse * (e_sq + lifted * cross_t) + t_sq
-    part_m[q] = row_sums(jnp.ones((8, quarter), BF), errors)[0:1]
-    for d in range(1, n_mp):
-        copy_m(d).start()
-    for d in range(1, n_mp):
-        arrive_m(d).wait_recv()
-    total = part_m[0]
-    for i in range(1, n_mp):
-        total = total + part_m[i]
-    fitness = -total / (tok * full)
-    fits[0] = fitness
-    for d in range(1, n_pop):
-        copy_f(d).start()
-    fit_out[...] = fitness
+    fits[0, q] = row_sums(jnp.ones((8, quarter), BF), errors)[0:1]
+    for i, j in peers:
+        copy_f(i, j).start()
     for d in range(1, n_pop):
         copy_l(d).wait_recv()
         copy_r(d).wait_recv()
@@ -335,9 +341,13 @@
     ceiling = math.log(members / 2 + 1)
     whole = sum(max(0.0, ceiling - math.log(i + 1.0)) for i in range(members))
     shaped = jnp.maximum(0.0, ceiling - jnp.log(uall[...] + 1.0)) / whole - 1.0 / members
-    for d in range(1, n_pop):
-        copy_f(d).wait_recv()
-    everyone = fits[...]
+    for i, j in peers:
+        arrive_f(i, j).wait_recv()
+    total = fits[:, 0]
+    for j in range(1, n_mp):
+        total = total + fits[:, j]
+    everyone = -total / (tok * full)
+    fit_out[...] = everyone[0]
     average = jnp.sum(jnp.sum(everyone, axis=0), axis=1, keepdims=True) / members
     centre = everyone - average[None]
     spread = jnp.sqrt(jnp.sum(jnp.sum(centre * centre, axis=0), axis=1, keepdims=True) / members + 1e-05)
@@ -358,12 +368,12 @@
     for d in range(1, n_mp):
         copy_pre(d).wait_send()
         copy_post(d).wait_send()
-        copy_m(d).wait_send()
     for d in range(1, n_pop):
         copy_l(d).wait_send()
         copy_r(d).wait_send()
         copy_u(d).wait_send()
-        copy_f(d).wait_send()
+    for i, j in peers:
+        copy_f(i, j).wait_send()
 
 
 def in_hbm(x):
@@ -394,7 +404,7 @@
             jax.ShapeDtypeStruct((n_pop * mem, width), BF),
             jax.ShapeDtypeStruct((1, mem), F32),
         ),
-        in_specs=[anywhere] * 4 + [vmem, anywhere, anywhere, vmem, vmem],
+        in_specs=[anywhere] * 8,
         out_specs=[vmem] * 4,
         scratch_shapes=[
             pltpu.VMEM((4, chunks, width, BLK), BF),
@@ -402,6 +412,9 @@
             pltpu.VMEM((tok, width), BF),
             pltpu.VMEM((tok, width), BF),
             pltpu.VMEM((mem, width), BF),
+            pltpu.VMEM((1, full), F32),
+            pltpu.VMEM((mem, full), BF),
+            pltpu.VMEM((1, mem), jnp.int32),
             block, block, block, block, block, block,
             pltpu.VMEM((n_pop, mem, rows), BF),
             pltpu.VMEM((n_pop, mem, width), BF),
@@ -412,63 +425,64 @@
             pltpu.VMEM((n_mp - 1, 2 * mem + 8, quarter), F32),
             pltpu.VMEM((n_mp, 2 * mem + 8, quarter), F32),
             pltpu.VMEM((n_mp - 1, 2 * mem + 8, quarter), F32),
-            pltpu.VMEM((n_mp, 1, mem), F32),
-            pltpu.VMEM((n_pop, 1, mem), F32),
+            pltpu.VMEM((n_pop, n_mp, 1, mem), F32),
             dma((4, chunks)),
-            dma((6,)),
+            dma((9,)),
         ]
         + [dma((chunks,))] * 6
-        + [dma((n_mp - 1,))] * 6
-        + [dma((n_pop - 1,))] * 8,
+        + [dma((n_mp - 1,))] * 4
+        + [dma((n_pop - 1,))] * 6
+        + [dma((n_mp * n_pop - 1,))] * 2,
         compiler_params=pltpu.CompilerParams(
             collective_id=0, has_side_effects=True, vmem_limit_bytes=48 * 1024 * 1024
         ),
     )(
-        *map(in_hbm, (context, out_weight, residual, target)), norm_gain.reshape(1, full),
-        in_hbm(left_factors), in_hbm(right_factors), right_factors, ranks,
+        *map(in_hbm, (
+            context, out_weight, residual, target, norm_gain.reshape(1, full), left_factors,
+            right_factors, ranks,
+        ))
     )
     count_all = n_pop * mem
-    steps = rows // 128
-    part = width // steps
     update, base, fitness = pl.pallas_call(
         functools.partial(finish, math.sqrt(count_all) / SIGMA),
         name="es_update",
-        grid=(steps,),
         out_shape=(
             jax.ShapeDtypeStruct((rows, width), F32),
             jax.ShapeDtypeStruct((tok, width), F32),
             jax.ShapeDtypeStruct((1, mem), F32),
         ),
-        in_specs=[
-            pl.BlockSpec((count_all, 128), lambda i: (0, i)),
-            pl.BlockSpec((count_all, width), lambda i: (0, 0)),
-            pl.BlockSpec((tok, part), lambda i: (0, i)),
-            pl.BlockSpec((1, mem), lambda i: (0, 0)),
-        ],
-        out_specs=(
-            pl.BlockSpec((128, width), lambda i: (i, 0)),
-            pl.BlockSpec((tok, part), lambda i: (0, i)),
-            pl.BlockSpec((1, mem), lambda i: (0, 0)),
-        ),
+        in_specs=[vmem] * 4,
+        out_specs=[anywhere] * 3,
+        scratch_shapes=[pltpu.VMEM((rows, width), F32), dma((rows // 128 + 2,))],
         compiler_params=pltpu.CompilerParams(vmem_limit_bytes=16 * 1024 * 1024),
     )(weighted, right_all, base, fitness)
     return (update, fitness.reshape(mem), base)
 
 
-def finish(scale, weighted, right_all, base_in, fit_in, update, base, fit):
-    update[...] = lax.dot_general(
-        weighted[...], right_all[...], (((0,), (0,)), ((), ())), preferred_element_type=F32
-    ) * scale
-    base[...] = base_in[...]
-    fit[...] = fit_in[...]
+def finish(scale, weighted, right_all, base_in, fit_in, update, base, fit, held, sems):
+    steps = held.shape[0] // 128
+    copies = [
+        pltpu.make_async_copy(base_in, base, sems.at[steps]),
+        pltpu.make_async_copy(fit_in, fit, sems.at[steps + 1]),
+    ]
+    copies[0].start()
+    copies[1].start()
+    for i in range(steps):
+        part = slice(i * 128, (i + 1) * 128)
+        held[part, :] = lax.dot_general(
+            weighted[:, part], right_all[...], (((0,), (0,)), ((), ())), preferred_element_type=F32
+        ) * scale
+        copies.append(pltpu.make_async_copy(held.at[part], update.at[part], sems.at[i]))
+        copies[-1].start()
+    for item in copies:
+        item.wait()
 
 
 def chosen(n_pop, n_mp, context, out_weight, *rest):
     tok, width = context.shape
     mem = rest[3].shape[0]
     full = out_weight.shape[1]
-    full_rows = full // n_pop
-    if n_mp == 4 and width % BLK == 0 and (full // n_pop) % 128 == 0 and tok % (16 * n_mp) == 0 and mem % 16 == 0 and width % full_rows == 0:
+    if n_mp == 4 and width % BLK == 0 and width > BLK and (full // n_pop) % 128 == 0 and tok % (16 * n_mp) == 0 and mem % 16 == 0:
         return fused_shards(n_pop, n_mp, context, out_weight, *rest)
     return shards(context, out_weight, *rest)
 

time: 52.4 us -> 45.4 us (0.87)
  Pallas kernels: 50.2 us -> 44.6 us
  local copies, waits for them, and re-layouts: 1.38 us -> 0 us
    pallas_call x1, Pallas kernels: 46.5 us -> 42.1 us  [fused_shards(): pl.pallas_call(functools.partial(kernel, n_pop, n_mp), name='es_step', ou...]
    unnamed x4 -> x0, local copies, waits for them, and re-layouts: 1.38 us -> none
    pallas_call x1, Pallas kernels: 3.76 us -> 2.43 us  [fused_shards(): pl.pallas_call(functools.partial(finish, math.sqrt(count_all) / SIGMA), n...]
where the time goes in v3:
time: 45.4 us; the launch traced here: 45.2 us
  Pallas kernels  44.6 us (98%)
  between operations  0.64 us (1%)
    pallas_call x1, Pallas kernels, fused_shards(): pl.pallas_call(functools.partial(kernel, n_pop, n_mp), name='es_step', ou...  42.1 us
    pallas_call x1, Pallas kernels, fused_shards(): pl.pallas_call(functools.partial(finish, math.sqrt(count_all) / SIGMA), n...  2.43 us

profile of v3, /device:TPU:0, one launch (start us, length us, event | category | flops | bytes accessed | tf_op | source)
XLA Modules:
  0.0 45.2 jit_solution(2857395583636637951)
XLA Ops:
  0.6 42.1 %es_step.1 = (f32[384,1280]{1,0:T(8,128)S(1)}, bf16[128,640]{1,0:T(8,128)(2,1)S(1)}, bf16[128,1280]{1,0:T(8,128)(2,1)S(1)}, f32[1,16]{1,0:T(1,128)S(1)}) custom-call(bf16[384,1280]{1,0:T(8,128)(2,1)} %ctx_h.1, bf16[1280,5120]{1,0:T(8,128)(2,1)} %w_h.1, bf16[384,1280]{1,0:T(8,128)(2,1)} %res_h.1, bf16[384,1280]{1,0:T(8,128)(2,1)} %tgt_h.1, ...), custom_call_target="tpu_custom_call" | custom-call | tf_op jit(solution)/shard_map/es_step/pallas_call | solution.py:398
  42.8 2.4 %es_update.1 = (f32[640,1280]{1,0:T(8,128)}, f32[384,1280]{1,0:T(8,128)}, f32[1,16]{1,0:T(1,128)}) custom-call(bf16[128,640]{1,0:T(8,128)(2,1)S(1)} %get-tuple-element.10.weighted, bf16[128,1280]{1,0:T(8,128)(2,1)S(1)} %get-tuple-element.11.right_all, f32[384,1280]{1,0:T(8,128)S(1)} %get-tuple-element.12.base_in, f32[1,16]{1,0:T(1,128)S(1)} %get-tuple-element.13.fit_in), custom_call_target="tpu_custom_call" | custom-call | tf_op jit(solution)/shard_map/es_update/pallas_call | solution.py:446

commit v4 on v3

--- a/solution.py
+++ b/solution.py
@@ -152,10 +152,9 @@
         pltpu.make_async_copy(right_h, right, loc_sem.at[7]),
         pltpu.make_async_copy(ranks_h, ranks, loc_sem.at[8]),
     ]
+    w_copy(0, 0).start()
     locals_[0].start()
-    for k in range(2):
-        for s in range(3):
-            w_copy(s, k).start()
+    w_copy(1, 0).start()
 
     barrier = pltpu.get_barrier_semaphore()
     peers = [(i, j) for i in range(n_pop) for j in range(n_mp)][1:]
@@ -206,7 +205,12 @@
         return jnp.dot(ctx[...], w_v[s, k], preferred_element_type=F32)
 
     locals_[0].wait()
-    send_a[0] = product(0, 0).astype(BF)
+    w_copy(0, 0).wait()
+    w_copy(0, 1).start()
+    w_copy(2, 0).start()
+    w_copy(1, 1).start()
+    w_copy(2, 1).start()
+    send_a[0] = jnp.dot(ctx[...], w_v[0, 0], preferred_element_type=F32).astype(BF)
     pl.semaphore_wait(barrier, n_mp * n_pop - 1)
     copy_a(0).start()
 

time: 45.4 us -> 44.9 us (0.989)
  Pallas kernels: 44.6 us -> 44.1 us
    pallas_call x1, Pallas kernels: 42.1 us -> 41.7 us  [fused_shards(): pl.pallas_call(functools.partial(kernel, n_pop, n_mp), name='es_step', ou...]
where the time goes in v4:
time: 44.9 us; the launch traced here: 44.7 us
  Pallas kernels  44.1 us (98%)
  between operations  0.64 us (1%)
    pallas_call x1, Pallas kernels, fused_shards(): pl.pallas_call(functools.partial(kernel, n_pop, n_mp), name='es_step', ou...  41.7 us
    pallas_call x1, Pallas kernels, fused_shards(): pl.pallas_call(functools.partial(finish, math.sqrt(count_all) / SIGMA), n...  2.43 us

profile of v4, /device:TPU:0, one launch (start us, length us, event | category | flops | bytes accessed | tf_op | source)
XLA Modules:
  0.0 44.7 jit_solution(1905156824356775182)
XLA Ops:
  0.6 41.7 %es_step.1 = (f32[384,1280]{1,0:T(8,128)S(1)}, bf16[128,640]{1,0:T(8,128)(2,1)S(1)}, bf16[128,1280]{1,0:T(8,128)(2,1)S(1)}, f32[1,16]{1,0:T(1,128)S(1)}) custom-call(bf16[384,1280]{1,0:T(8,128)(2,1)} %ctx_h.1, bf16[1280,5120]{1,0:T(8,128)(2,1)} %w_h.1, bf16[384,1280]{1,0:T(8,128)(2,1)} %res_h.1, bf16[384,1280]{1,0:T(8,128)(2,1)} %tgt_h.1, ...), custom_call_target="tpu_custom_call" | custom-call | tf_op jit(solution)/shard_map/es_step/pallas_call | solution.py:402
  42.3 2.4 %es_update.1 = (f32[640,1280]{1,0:T(8,128)}, f32[384,1280]{1,0:T(8,128)}, f32[1,16]{1,0:T(1,128)}) custom-call(bf16[128,640]{1,0:T(8,128)(2,1)S(1)} %get-tuple-element.10.weighted, bf16[128,1280]{1,0:T(8,128)(2,1)S(1)} %get-tuple-element.11.right_all, f32[384,1280]{1,0:T(8,128)S(1)} %get-tuple-element.12.base_in, f32[1,16]{1,0:T(1,128)S(1)} %get-tuple-element.13.fit_in), custom_call_target="tpu_custom_call" | custom-call | tf_op jit(solution)/shard_map/es_update/pallas_call | solution.py:450

commit v5 on v4

--- a/solution.py
+++ b/solution.py
@@ -262,15 +262,17 @@
     gain_mine = gain[:, my_cols]
     r_mine = rall[0].astype(F32)
     gr_hi, gr_lo = split_two(r_mine * gain_mine)
+    squares = jnp.zeros((quarter, 128), F32)
     for t in range(n_mp):
         part = slice(t * quarter, (t + 1) * quarter)
         target = tgt[part, :]
         pre[t, 0:mem, :] = nt_dot(lcols[...], ctx[part, :])
         pre[t, mem:2 * mem, :] = nt_dot(gr_hi, target) + nt_dot(gr_lo, target)
         wide = target.astype(F32)
-        pre[t, 2 * mem:2 * mem + 8, :] = row_sums(ones, fold_lanes(wide * wide))
+        squares = squares + fold_lanes(wide * wide)
     for d in range(1, n_mp):
         copy_pre(d).start()
+    t_sq = jnp.sum(jnp.sum(squares, axis=1, keepdims=True), axis=0, keepdims=True)
     g2_hi, g2_lo = split_two(r_mine * (gain_mine * gain_mine))
     for k in range(chunks):
         cols = slice(k * BLK, (k + 1) * BLK)
@@ -323,7 +325,6 @@
         late = late + post_in[d - 1]
     lifted = early[0:mem] * (SIGMA / math.sqrt(full))
     cross_t = early[mem:2 * mem]
-    t_sq = early[2 * mem:2 * mem + 1]
     crossed = late[0:mem]
     crossed_g = late[mem:2 * mem]
     s_sq = late[2 * mem:2 * mem + 1]
@@ -332,8 +333,8 @@
     meansq = (s_sq + 2.0 * lifted * crossed + lifted * lifted * norm_r) / full
     inverse = lax.rsqrt(meansq + EPSILON)
     power = a_sq + 2.0 * lifted * crossed_g + lifted * lifted * norm_gr
-    errors = inverse * inverse * power - 2.0 * inverse * (e_sq + lifted * cross_t) + t_sq
-    fits[0, q] = row_sums(jnp.ones((8, quarter), BF), errors)[0:1]
+    errors = inverse * inverse * power - 2.0 * inverse * (e_sq + lifted * cross_t)
+    fits[0, q] = row_sums(jnp.ones((8, quarter), BF), errors)[0:1] + t_sq
     for i, j in peers:
         copy_f(i, j).start()
     for d in range(1, n_pop):
@@ -425,8 +426,8 @@
             pltpu.VMEM((n_pop, 1, mem), F32),
             pltpu.VMEM((chunks, 3 * mem, BLK), BF),
             acc, acc, acc,
-            pltpu.VMEM((n_mp, 2 * mem + 8, quarter), F32),
-            pltpu.VMEM((n_mp - 1, 2 * mem + 8, quarter), F32),
+            pltpu.VMEM((n_mp, 2 * mem, quarter), F32),
+            pltpu.VMEM((n_mp - 1, 2 * mem, quarter), F32),
             pltpu.VMEM((n_mp, 2 * mem + 8, quarter), F32),
             pltpu.VMEM((n_mp - 1, 2 * mem + 8, quarter), F32),
             pltpu.VMEM((n_pop, n_mp, 1, mem), F32),

time: 44.9 us -> 44.9 us (level)
  no operation moved by 1% of the time
where the time goes in v5:
time: 44.9 us; the launch traced here: 44.7 us
  Pallas kernels  44.1 us (98%)
  between operations  0.64 us (1%)
    pallas_call x1, Pallas kernels, fused_shards(): pl.pallas_call(functools.partial(kernel, n_pop, n_mp), name='es_step', ou...  41.7 us
    pallas_call x1, Pallas kernels, fused_shards(): pl.pallas_call(functools.partial(finish, math.sqrt(count_all) / SIGMA), n...  2.43 us

profile of v5, /device:TPU:0, one launch (start us, length us, event | category | flops | bytes accessed | tf_op | source)
XLA Modules:
  0.0 44.7 jit_solution(17526375982216431992)
XLA Ops:
  0.6 41.7 %es_step.1 = (f32[384,1280]{1,0:T(8,128)S(1)}, bf16[128,640]{1,0:T(8,128)(2,1)S(1)}, bf16[128,1280]{1,0:T(8,128)(2,1)S(1)}, f32[1,16]{1,0:T(1,128)S(1)}) custom-call(bf16[384,1280]{1,0:T(8,128)(2,1)} %ctx_h.1, bf16[1280,5120]{1,0:T(8,128)(2,1)} %w_h.1, bf16[384,1280]{1,0:T(8,128)(2,1)} %res_h.1, bf16[384,1280]{1,0:T(8,128)(2,1)} %tgt_h.1, ...), custom_call_target="tpu_custom_call" | custom-call | tf_op jit(solution)/shard_map/es_step/pallas_call | solution.py:403
  42.3 2.4 %es_update.1 = (f32[640,1280]{1,0:T(8,128)}, f32[384,1280]{1,0:T(8,128)}, f32[1,16]{1,0:T(1,128)}) custom-call(bf16[128,640]{1,0:T(8,128)(2,1)S(1)} %get-tuple-element.10.weighted, bf16[128,1280]{1,0:T(8,128)(2,1)S(1)} %get-tuple-element.11.right_all, f32[384,1280]{1,0:T(8,128)S(1)} %get-tuple-element.12.base_in, f32[1,16]{1,0:T(1,128)S(1)} %get-tuple-element.13.fit_in), custom_call_target="tpu_custom_call" | custom-call | tf_op jit(solution)/shard_map/es_update/pallas_call | solution.py:451
